TPU v7x, 256 devices: a whole 4x4x8 slice. The times are simulated.
256 devices in a mesh: row: 8 (over x, core), col: 32 (over z, y).
Axes of the slice: x: 4, y: 4, z: 8, core: 2. Of those that a mesh axis runs over, the one named last changes fastest.
Arguments:
- inputs: bfloat16 [1024, 8192], P('col', 'row'), may hold values from -6 to 6
- target: bfloat16 [1024, 8192], P(None, 'row'), may hold values from -6 to 6
- gate_weight: bfloat16 [8192, 16384], P('row', 'col'), may hold values from -0.0625 to 0.0625
- up_weight: bfloat16 [8192, 16384], P('row', 'col'), may hold values from -0.0625 to 0.0625
- down_weight: bfloat16 [16384, 8192], P('col', 'row'), may hold values from -0.046875 to 0.046875
Outputs:
- output: bfloat16 [1024, 8192], P('col', 'row')
- grad_inputs: bfloat16 [1024, 8192], P('col', 'row')
- grad_gate_weight: bfloat16 [8192, 16384], P('row', 'col')
- grad_up_weight: bfloat16 [8192, 16384], P('row', 'col')
- grad_down_weight: bfloat16 [16384, 8192], P('col', 'row')
All inputs are finite; a program needn't handle non-finite values.
Results may differ from a plain program's by a relative error of at most 0.0065.
Values may be sent and summed in bfloat16 or wider, within the bound.
No kernel may reach another device: no remote copies, remote signals or barrier semaphores. Data moves between devices by JAX's collectives and lax.ppermute only.
A program may use at most 64 MiB of HBM per device.

v0:
```python
import jax
import jax.numpy as jnp
from jax import lax
from jax.sharding import Mesh, PartitionSpec as P

F32 = jnp.float32
BF16 = jnp.bfloat16
NX, NC, NZ, NY = (4, 2, 8, 4)


def contract_first(left, right):
    return lax.dot_general(left, right, (((0,), (0,)), ((), ())), preferred_element_type=F32)


def contract_last(left, right):
    return lax.dot_general(left, right, (((1,), (1,)), ((), ())), preferred_element_type=F32)


def exchange(val, axis):
    return lax.all_to_all(val, axis, split_axis=0, concat_axis=0, tiled=True)


def scatter_sum(part, axis, size):
    rows, cols = part.shape
    got = exchange(part.astype(BF16), axis).reshape(size, rows // size, cols)
    return jnp.sum(got.astype(F32), axis=0)


def spread(own, axis, size):
    rows, cols = own.shape
    return exchange(
        jnp.broadcast_to(own[None], (size, rows, cols)).reshape(size * rows, cols), axis
    )


def gather_col(own):
    return lax.all_gather(spread(own, "z", NZ), "y", axis=0, tiled=True)


def scatter_col(part):
    return scatter_sum(scatter_sum(part, "y", NY), "z", NZ)


def swap_core(val):
    return lax.ppermute(val, "core", [(0, 1), (1, 0)])


def scatter_row(part):
    half = part.shape[0] // NC
    core = lax.axis_index("core")
    mine = lax.dynamic_slice_in_dim(part, core * half, half, 0)
    other = lax.dynamic_slice_in_dim(part, (1 - core) * half, half, 0)
    both = mine + swap_core(other.astype(BF16)).astype(F32)
    return scatter_sum(both, "x", NX)


def gather_row(own):
    mine = spread(own, "x", NX)
    other = swap_core(mine)
    first = lax.axis_index("core") == 0
    return jnp.concatenate([jnp.where(first, mine, other), jnp.where(first, other, mine)], axis=0)


def gate_grads(hidden_grad, gate_act, up_act):
    sigma = jax.nn.sigmoid(gate_act)
    silu_val = gate_act * sigma
    grad_gate = hidden_grad * up_act * sigma * (1.0 + gate_act * (1.0 - sigma))
    grad_up = hidden_grad * silu_val
    return jnp.concatenate([grad_gate.astype(BF16), grad_up.astype(BF16)], axis=1)


def body(inputs, target, gate_weight, up_weight, down_weight):
    wide = gate_weight.shape[1]
    tok_own = inputs.shape[0]
    tokens_all = gather_col(inputs)
    gate_part = jnp.dot(tokens_all, gate_weight, preferred_element_type=F32)
    up_part = jnp.dot(tokens_all, up_weight, preferred_element_type=F32)
    acts = scatter_row(jnp.concatenate([gate_part, up_part], axis=1))
    gate_own, up_own = (acts[:, :wide], acts[:, wide:])
    hidden_own = (jax.nn.silu(gate_own) * up_own).astype(BF16)
    hidden_all = gather_row(hidden_own)
    result_part = jnp.dot(hidden_all, down_weight, preferred_element_type=F32)
    result_own = scatter_col(result_part)
    offset = (lax.axis_index("z") * NY + lax.axis_index("y")) * tok_own
    target_own = lax.dynamic_slice_in_dim(target, offset, tok_own, 0)
    error_own = (result_own - target_own.astype(F32)).astype(BF16)
    output = result_own.astype(BF16)
    error_all = gather_col(error_own)
    hidden_grad = scatter_row(contract_last(error_all, down_weight))
    grads_all = gather_row(gate_grads(hidden_grad, gate_own, up_own))
    gate_grad_all, up_grad_all = (grads_all[:, :wide], grads_all[:, wide:])
    input_grad_part = contract_last(gate_grad_all, gate_weight) + contract_last(
        up_grad_all, up_weight
    )
    grad_inputs = scatter_col(input_grad_part).astype(BF16)
    grad_down_weight = contract_first(hidden_all, error_all).astype(BF16)
    grad_gate_weight = contract_first(tokens_all, gate_grad_all).astype(BF16)
    grad_up_weight = contract_first(tokens_all, up_grad_all).astype(BF16)
    return (output, grad_inputs, grad_gate_weight, grad_up_weight, grad_down_weight)


def solution(mesh):
    fine = Mesh(mesh.devices.reshape(NX, NC, NZ, NY), ("x", "core", "z", "y"))
    row, col = (("x", "core"), ("z", "y"))
    placed = (P(col, row), P(None, row), P(row, col), P(row, col), P(col, row))
    return jax.shard_map(
        body,
        mesh=fine,
        in_specs=placed,
        out_specs=(P(col, row), P(col, row), P(row, col), P(row, col), P(col, row)),
        check_vma=False,
    )
```

profile of v0, /device:TPU:1, one launch (start us, length us, event | category | flops | bytes accessed | tf_op | source)
XLA Modules:
  0.0 317.7 jit_solution(8181957383931177860)
XLA Ops:
  7.2 0.0 copy-start
  7.2 0.0 all-gather.3.cloned.1.call-start
  7.2 1.0 broadcast_in_dim.8
  8.2 25.0 %all_to_all.90 = bf16[8,32,1024]{2,1,0:T(8,128)(2,1)} all-to-all(bf16[8,32,1024]{2,1,0:T(8,128)(2,1)S(1)} %broadcast_in_dim.8), channel_id=1, replica_groups=mesh['x'=4,'core'=2,'z'=8,'y'=4] {'z'}, dimensions={0} | all-to-all | bytes 1048576 | tf_op jit(solution)/shard_map/all_to_all | solution.py:20
  33.2 0.0 all-gather.3.cloned.1.call-update
  33.3 31.3 %all-gather.3.cloned.1.call-done = bf16[1024,1024]{1,0:T(8,128)(2,1)} async-done(((bf16[256,1024]{1,0:T(8,128)(2,1)}), bf16[1024,1024]{1,0:T(8,128)(2,1)}) %all-gather.3.cloned.1.call-update) | async-done | bytes 2097168 | tf_op jit(solution)/shard_map/all_gather | solution.py:37
  64.6 3.3 %fusion.18 = f32[1024,512]{0,1:T(8,128)S(1)} fusion(bf16[1024,1024]{1,0:T(8,128)(2,1)} %all-gather.3.cloned.1.call-done, bf16[1024,512]{1,0:T(8,128)(2,1)} %param.8), kind=kOutput, calls=%fused_computation.45 | convolution fusion | flops 1073741824 | bytes 5242880 | tf_op jit(solution)/shard_map/dot_general | solution.py:77
  67.9 1.3 fusion.17
  69.2 1.3 fusion.1
  70.5 0.4 copy-done.1
  70.9 0.8 collective-permute-start
  71.8 2.6 collective-permute-done
  74.4 1.7 copy_bitcast_fusion
  76.2 18.0 %all_to_all.91 = bf16[4,128,1024]{1,2,0:T(8,128)(2,1)S(1)} all-to-all(bf16[4,128,1024]{1,2,0:T(8,128)(2,1)S(1)} %copy_bitcast_fusion), channel_id=1, replica_groups=mesh['x'=4,'core'=2,'z'=8,'y'=4] {'x'}, dimensions={0} | all-to-all | bytes 2097152 | tf_op jit(solution)/shard_map/all_to_all | solution.py:20
  94.2 0.1 convert_reduce_fusion
  94.3 0.0 copy-start.2
  94.3 0.8 copy-done.2
  95.1 0.1 multiply_convert_fusion.2
  95.2 0.1 copy.28
  95.4 10.2 %all_to_all.92 = bf16[4,128,512]{2,1,0:T(8,128)(2,1)S(1)} all-to-all(bf16[4,128,512]{2,1,0:T(8,128)(2,1)S(1)} %broadcast_in_dim.9), channel_id=1, replica_groups=mesh['x'=4,'core'=2,'z'=8,'y'=4] {'x'}, dimensions={0} | all-to-all | bytes 1048576 | tf_op jit(solution)/shard_map/all_to_all | solution.py:20
  105.5 2.7 collective-permute-start.1
  108.2 1.5 collective-permute-done.1
  109.7 0.1 broadcast_select_fusion.3
  109.9 0.0 copy-start.10
  109.9 1.3 convolution_convert_fusion
  111.2 28.0 %all_to_all.93 = bf16[4,256,1024]{2,1,0:T(8,128)(2,1)S(1)} all-to-all(bf16[4,256,1024]{2,1,0:T(8,128)(2,1)S(1)} %bitcast.38), channel_id=1, replica_groups=mesh['x'=4,'core'=2,'z'=8,'y'=4] {'y'}, dimensions={0} | all-to-all | bytes 4194304 | tf_op jit(solution)/shard_map/all_to_all | solution.py:20
  139.2 1.3 reduce_sum.64
  140.5 6.7 %all-to-all-start.4 = ((bf16[8,32,1024]{2,1,0:T(8,128)(2,1)}), bf16[8,32,1024]{2,1,0:T(8,128)(2,1)S(1)}, u32[]{:S(2)}, u32[]{:S(2)}) async-start(bf16[8,32,1024]{2,1,0:T(8,128)(2,1)} %bitcast.41), calls=%async_computation.4 | async-start | bytes 1048576 | tf_op jit(solution)/shard_map/all_to_all | solution.py:20
  147.2 0.0 all-gather.5.cloned.1.call-start
  147.3 15.7 %all-to-all-done.4 = bf16[8,32,1024]{2,1,0:T(8,128)(2,1)S(1)} async-done(((bf16[8,32,1024]{2,1,0:T(8,128)(2,1)}), bf16[8,32,1024]{2,1,0:T(8,128)(2,1)S(1)}, u32[]{:S(2)}, u32[]{:S(2)}) %all-to-all-start.4) | async-done | bytes 524320 | tf_op jit(solution)/shard_map/all_to_all | solution.py:20
  163.0 0.1 convert_reduce_fusion.2
  163.0 1.5 subtract_convert_fusion
  164.6 17.5 %all_to_all.94 = bf16[8,32,1024]{2,1,0:T(8,128)(2,1)} all-to-all(bf16[8,32,1024]{2,1,0:T(8,128)(2,1)S(1)} %broadcast_in_dim.10), channel_id=1, replica_groups=mesh['x'=4,'core'=2,'z'=8,'y'=4] {'z'}, dimensions={0} | all-to-all | bytes 1048576 | tf_op jit(solution)/shard_map/all_to_all | solution.py:20
  182.1 0.0 all-gather.5.cloned.1.call-update
  182.2 29.1 %all-gather.5.cloned.1.call-done = bf16[1024,1024]{1,0:T(8,128)(2,1)} async-done(((bf16[256,1024]{1,0:T(8,128)(2,1)}), bf16[1024,1024]{1,0:T(8,128)(2,1)}) %all-gather.5.cloned.1.call-update) | async-done | bytes 2097168 | tf_op jit(solution)/shard_map/all_gather | solution.py:37
  211.3 2.9 fusion.19
  214.1 0.1 dynamic-slice_convert_fusion
  214.2 0.0 copy-start.3
  214.2 0.9 collective-permute-start.2
  215.2 1.5 collective-permute-done.2
  216.7 0.2 add_convert_fusion.1
  216.9 12.4 %all_to_all.95 = bf16[4,128,512]{2,1,0:T(8,128)(2,1)S(1)} all-to-all(bf16[4,128,512]{2,1,0:T(8,128)(2,1)S(1)} %bitcast.37), channel_id=1, replica_groups=mesh['x'=4,'core'=2,'z'=8,'y'=4] {'x'}, dimensions={0} | all-to-all | bytes 1048576 | tf_op jit(solution)/shard_map/all_to_all | solution.py:20
  229.3 0.1 convert_reduce_fusion.1
  229.4 0.1 copy.29
  229.5 0.2 multiply_convert_fusion.1
  229.7 0.1 copy.31
  229.9 0.1 broadcast_in_dim.11
  230.0 15.8 %all_to_all.96 = bf16[4,128,1024]{2,1,0:T(8,128)(2,1)S(1)} all-to-all(bf16[4,128,1024]{2,1,0:T(8,128)(2,1)S(1)} %broadcast_in_dim.11), channel_id=1, replica_groups=mesh['x'=4,'core'=2,'z'=8,'y'=4] {'x'}, dimensions={0} | all-to-all | bytes 2097152 | tf_op jit(solution)/shard_map/all_to_all | solution.py:20
  245.8 2.7 collective-permute-start.3
  248.5 2.3 collective-permute-done.3
  250.7 0.2 broadcast_select_fusion.1
  251.0 0.0 copy-start.8
  251.0 1.3 fusion.10
  252.3 1.3 add_convert_fusion
  253.6 29.3 %all_to_all.97 = bf16[4,256,1024]{2,1,0:T(8,128)(2,1)} all-to-all(bf16[4,256,1024]{2,1,0:T(8,128)(2,1)S(1)} %bitcast.34), channel_id=1, replica_groups=mesh['x'=4,'core'=2,'z'=8,'y'=4] {'y'}, dimensions={0} | all-to-all | bytes 4194304 | tf_op jit(solution)/shard_map/all_to_all | solution.py:20
  282.8 2.9 reduce_sum.67
  285.8 6.7 %all-to-all-start.9 = ((bf16[8,32,1024]{2,1,0:T(8,128)(2,1)}), bf16[8,32,1024]{2,1,0:T(8,128)(2,1)}, u32[]{:S(2)}, u32[]{:S(2)}) async-start(bf16[8,32,1024]{2,1,0:T(8,128)(2,1)} %bitcast.42), calls=%async_computation.9 | async-start | bytes 1048576 | tf_op jit(solution)/shard_map/all_to_all | solution.py:20
  292.5 4.3 %convolution_convert_fusion.1 = bf16[512,1024]{1,0:T(8,128)(2,1)} fusion(bf16[1024,1024]{1,0:T(8,128)(2,1)} %all-gather.5.cloned.1.call-done, bf16[512,512]{1,0:T(8,128)(2,1)} %copy-done.10, bf16[512,512]{1,0:T(8,128)(2,1)} %copy-done.9), kind=kOutput, calls=%fused_computation.14 | convolution fusion | flops 1076363264 | bytes 4194304 | tf_op jit(solution)/shard_map/dot_general | solution.py:12
  296.8 2.2 fusion.6
  299.1 2.3 copy.33
  301.4 3.9 %fusion.5 = bf16[1024,512]{0,1:T(8,128)(2,1)} fusion(bf16[1024,1024]{1,0:T(8,128)(2,1)} %all-gather.3.cloned.1.call-done, bf16[512,1024]{1,0:T(8,128)(2,1)S(1)} %get-tuple-element.25, bf16[512,1024]{1,0:T(8,128)(2,1)S(1)} %get-tuple-element.26), kind=kOutput, calls=%fused_computation.17 | convolution fusion | flops 1076363264 | bytes 5242880 | tf_op jit(solution)/shard_map/dot_general | solution.py:12
  305.2 2.3 copy.32
  307.5 1.6 all-to-all-done.9
  309.1 1.8 reduce_sum.68
  (18 shorter events, 0.1 us)
Async XLA Ops:
  7.2 102.7 %copy-start = (bf16[512,1024]{1,0:T(8,128)(2,1)S(1)}, bf16[512,1024]{1,0:T(8,128)(2,1)}, u32[]{:S(2)}) copy-start(bf16[512,1024]{1,0:T(8,128)(2,1)} %param.9) | copy-start | bytes 3145732
  7.2 57.4 %all-gather.3.cloned.1.call-start = ((), (), s32[]{:S(2)}) async-start(), calls=%async_computation.10 | async-start | bytes 2621440 | tf_op jit(solution)/shard_map/all_gather | solution.py:37
  64.6 3.3 %copy-start.4 = (bf16[1024,1024]{1,0:T(8,128)(2,1)S(1)}, bf16[1024,1024]{1,0:T(8,128)(2,1)}, u32[]{:S(2)}) copy-start(bf16[1024,1024]{1,0:T(8,128)(2,1)} %all-gather.3.cloned.1.call-done) | copy-start | bytes 6291460
  64.6 3.3 %copy-start.7 = (bf16[1024,512]{1,0:T(8,128)(2,1)S(1)}, bf16[1024,512]{1,0:T(8,128)(2,1)}, u32[]{:S(2)}) copy-start(bf16[1024,512]{1,0:T(8,128)(2,1)} %param.7) | copy-start | bytes 3145732
  69.2 1.7 copy-start.1
  70.9 3.5 %collective-permute-start = (bf16[512,1024]{0,1:T(8,128)(2,1)}, bf16[512,1024]{0,1:T(8,128)(2,1)}, u32[]{:S(2)}, u32[]{:S(2)}) collective-permute-start(bf16[512,1024]{0,1:T(8,128)(2,1)} %fusion.1), channel_id=1, source_target_pairs={{0,32},{32,0},{1,33},{33,1},{2,34},{34,2},{3,35},{35,3},{4,36},{36... | collective-permute-start | bytes 3145736 | tf_op jit(solution)/shard_map/ppermute | solution.py:45
  94.3 0.8 copy-start.2
  105.5 4.2 %collective-permute-start.1 = (bf16[512,512]{1,0:T(8,128)(2,1)S(1)}, bf16[512,512]{1,0:T(8,128)(2,1)S(1)}, u32[]{:S(2)}, u32[]{:S(2)}) collective-permute-start(bf16[512,512]{1,0:T(8,128)(2,1)S(1)} %bitcast.36), channel_id=1, source_target_pairs={{0,32},{32,0},{1,33},{33,1},{2,34},{34,2},{3,35},{35,3},{4,36},{36... | collective-permute-start | bytes 1572872 | tf_op jit(solution)/shard_map/ppermute | solution.py:45
  109.8 1.3 copy-start.9
  109.9 1.3 copy-start.10
  140.5 22.5 %all-to-all-start.4 = ((bf16[8,32,1024]{2,1,0:T(8,128)(2,1)}), bf16[8,32,1024]{2,1,0:T(8,128)(2,1)S(1)}, u32[]{:S(2)}, u32[]{:S(2)}) async-start(bf16[8,32,1024]{2,1,0:T(8,128)(2,1)} %bitcast.41), calls=%async_computation.4 | async-start | bytes 1048576 | tf_op jit(solution)/shard_map/all_to_all | solution.py:20
  147.2 64.1 %all-gather.5.cloned.1.call-start = ((), (), s32[]{:S(2)}) async-start(), calls=%async_computation.11 | async-start | bytes 2621440 | tf_op jit(solution)/shard_map/all_gather | solution.py:37
  214.2 15.3 %copy-start.3 = (f32[128,1024]{0,1:T(8,128)S(1)}, f32[128,1024]{0,1:T(8,128)}, u32[]{:S(2)}) copy-start(f32[128,1024]{0,1:T(8,128)} %copy-done.2) | copy-start | bytes 1572868
  214.2 2.5 collective-permute-start.2
  245.8 5.2 %copy-start.6 = (bf16[1024,512]{1,0:T(8,128)(2,1)S(1)}, bf16[1024,512]{1,0:T(8,128)(2,1)}, u32[]{:S(2)}) copy-start(bf16[1024,512]{1,0:T(8,128)(2,1)} %param.8) | copy-start | bytes 3145732
  245.8 4.9 %collective-permute-start.3 = (bf16[512,1024]{1,0:T(8,128)(2,1)S(1)}, bf16[512,1024]{1,0:T(8,128)(2,1)S(1)}, u32[]{:S(2)}, u32[]{:S(2)}) collective-permute-start(bf16[512,1024]{1,0:T(8,128)(2,1)S(1)} %bitcast.35), channel_id=1, source_target_pairs={{0,32},{32,0},{1,33},{33,1},{2,34},{34,2},{3,35},{35,3},{4,36},{36... | collective-permute-start | bytes 3145736 | tf_op jit(solution)/shard_map/ppermute | solution.py:45
  251.0 1.3 copy-start.8
  285.8 23.3 %all-to-all-start.9 = ((bf16[8,32,1024]{2,1,0:T(8,128)(2,1)}), bf16[8,32,1024]{2,1,0:T(8,128)(2,1)}, u32[]{:S(2)}, u32[]{:S(2)}) async-start(bf16[8,32,1024]{2,1,0:T(8,128)(2,1)} %bitcast.42), calls=%async_computation.9 | async-start | bytes 1048576 | tf_op jit(solution)/shard_map/all_to_all | solution.py:20
  292.5 4.3 %copy-start.5 = (bf16[1024,1024]{1,0:T(8,128)(2,1)S(1)}, bf16[1024,1024]{1,0:T(8,128)(2,1)}, u32[]{:S(2)}) copy-start(bf16[1024,1024]{1,0:T(8,128)(2,1)} %all-gather.3.cloned.1.call-done) | copy-start | bytes 6291460
Sparse Core Ops, SparseCore 0:
  33.4 31.1 all-gather.2
  182.3 28.9 all-gather.4
where the time goes:
time: 319 us; the launch traced here: 318 us
  blocking collectives  156 us (49%)
  waiting for transfers between devices  85.8 us (27%)
  matrix products  21.7 us (7%)
  starting transfers between devices  20.7 us (6%)
  between operations  14.3 us (4%)
  other arithmetic  11.6 us (4%)
  local copies, waits for them, and re-layouts  7.41 us (2%)
    all_to_all x8, blocking collectives, exchange(): return lax.all_to_all(val, axis, split_axis=0, concat_axis=0, tiled=True)  156 us
    all_gather x2, waiting for transfers between devices, gather_col(): return lax.all_gather(spread(own, 'z', NZ), 'y', axis=0, tiled=True)  60.5 us
    all_to_all x2, waiting for transfers between devices, exchange(): return lax.all_to_all(val, axis, split_axis=0, concat_axis=0, tiled=True)  17.3 us
    all_to_all x2, starting transfers between devices, exchange(): return lax.all_to_all(val, axis, split_axis=0, concat_axis=0, tiled=True)  13.5 us
    dot_general x3, matrix products, contract_first(): lax.dot_general(left, right, (((0,), (0,)), ((), ())), preferred_element_...  10.4 us
    ppermute x4, waiting for transfers between devices, swap_core(): return lax.ppermute(val, 'core', [(0, 1), (1, 0)])  7.99 us
    ppermute x4, starting transfers between devices, swap_core(): return lax.ppermute(val, 'core', [(0, 1), (1, 0)])  7.1 us
  transfers between devices with their start and end apart: 8, of which 8 were waited for; matrix products, arithmetic and copies ran while one was open for 5% of the time, Pallas kernels for 0%

commit v1 on v0

--- a/solution.py
+++ b/solution.py
@@ -34,7 +34,9 @@
 
 
 def gather_col(own):
-    return lax.all_gather(spread(own, "z", NZ), "y", axis=0, tiled=True)
+    return jnp.concatenate(
+        lax.all_to_all(jnp.stack(lax.axis_size("y") * [spread(own, "z", NZ)]), "y", 0, 0), 0
+    )
 
 
 def scatter_col(part):

time: 319 us -> 302 us (0.947)
  waiting for transfers between devices: 85.8 us -> 50.8 us
  blocking collectives: 156 us -> 183 us
  between operations: 14.3 us -> 0.95 us
  starting transfers between devices: 20.7 us -> 24 us
    all_gather x2 -> x0, waiting for transfers between devices: 60.5 us -> none  [gather_col(): return lax.all_gather(spread(own, 'z', NZ), 'y', axis=0, tiled=True)]
    all_to_all x0 -> x1, blocking collectives: none -> 25.9 us  [gather_col(): lax.all_to_all(jnp.stack(lax.axis_size('y') * [spread(own, 'z', NZ)]), 'y...]
    all_to_all x0 -> x1, waiting for transfers between devices: none -> 23.8 us  [gather_col(): lax.all_to_all(jnp.stack(lax.axis_size('y') * [spread(own, 'z', NZ)]), 'y...]
    all_to_all x2, starting transfers between devices: 13.5 us -> 7.63 us  [exchange(): return lax.all_to_all(val, axis, split_axis=0, concat_axis=0, tiled=True)]
    ppermute x4, starting transfers between devices: 7.1 us -> 12.2 us  [swap_core(): return lax.ppermute(val, 'core', [(0, 1), (1, 0)])]
    all_to_all x0 -> x1, starting transfers between devices: none -> 4.18 us  [gather_col(): lax.all_to_all(jnp.stack(lax.axis_size('y') * [spread(own, 'z', NZ)]), 'y...]
    unnamed x24 -> x28, local copies, waits for them, and re-layouts: 5.78 us -> 7.07 us
  transfers between devices with their start and end apart: 8 -> 7, of which waited for: 8 -> 7; matrix products, arithmetic and copies ran while one was open for 5% -> 5% of each run, Pallas kernels for 0% -> 0%
where the time goes in v1:
time: 302 us; the launch traced here: 301 us
  blocking collectives  183 us (61%)
  waiting for transfers between devices  50.8 us (17%)
  starting transfers between devices  24 us (8%)
  matrix products  20.1 us (7%)
  other arithmetic  11.6 us (4%)
  local copies, waits for them, and re-layouts  10.6 us (4%)
    all_to_all x8, blocking collectives, exchange(): return lax.all_to_all(val, axis, split_axis=0, concat_axis=0, tiled=True)  157 us
    all_to_all x1, blocking collectives, gather_col(): lax.all_to_all(jnp.stack(lax.axis_size('y') * [spread(own, 'z', NZ)]), 'y...  25.9 us
    all_to_all x1, waiting for transfers between devices, gather_col(): lax.all_to_all(jnp.stack(lax.axis_size('y') * [spread(own, 'z', NZ)]), 'y...  23.8 us
    all_to_all x2, waiting for transfers between devices, exchange(): return lax.all_to_all(val, axis, split_axis=0, concat_axis=0, tiled=True)  19 us
    ppermute x4, starting transfers between devices, swap_core(): return lax.ppermute(val, 'core', [(0, 1), (1, 0)])  12.2 us
    dot_general x3, matrix products, contract_first(): lax.dot_general(left, right, (((0,), (0,)), ((), ())), preferred_element_...  10.4 us
    ppermute x4, waiting for transfers between devices, swap_core(): return lax.ppermute(val, 'core', [(0, 1), (1, 0)])  7.99 us
    all_to_all x2, starting transfers between devices, exchange(): return lax.all_to_all(val, axis, split_axis=0, concat_axis=0, tiled=True)  7.63 us
  transfers between devices with their start and end apart: 7, of which 7 were waited for; matrix products, arithmetic and copies ran while one was open for 5% of the time, Pallas kernels for 0%

profile of v1, /device:TPU:1, one launch (start us, length us, event | category | flops | bytes accessed | tf_op | source)
XLA Modules:
  0.0 301.0 jit_solution(4285362848797881154)
XLA Ops:
  0.6 0.0 copy-start
  0.6 1.0 broadcast_in_dim.8
  1.6 24.9 %all_to_all.94 = bf16[8,32,1024]{2,1,0:T(8,128)(2,1)S(1)} all-to-all(bf16[8,32,1024]{2,1,0:T(8,128)(2,1)S(1)} %broadcast_in_dim.8), channel_id=1, replica_groups=mesh['x'=4,'core'=2,'z'=8,'y'=4] {'z'}, dimensions={0} | all-to-all | bytes 1048576 | tf_op jit(solution)/shard_map/all_to_all | solution.py:20
  26.5 1.6 stack.9
  28.2 4.2 %all-to-all-start.1 = ((bf16[4,256,1024]{2,1,0:T(8,128)(2,1)}), bf16[4,256,1024]{2,1,0:T(8,128)(2,1)S(1)}, u32[]{:S(2)}, u32[]{:S(2)}) async-start(bf16[4,256,1024]{2,1,0:T(8,128)(2,1)} %stack.9), calls=%async_computation.1 | async-start | bytes 4194304 | tf_op jit(solution)/shard_map/all_to_all | solution.py:38
  32.4 23.8 %all-to-all-done.1 = bf16[4,256,1024]{2,1,0:T(8,128)(2,1)S(1)} async-done(((bf16[4,256,1024]{2,1,0:T(8,128)(2,1)}), bf16[4,256,1024]{2,1,0:T(8,128)(2,1)S(1)}, u32[]{:S(2)}, u32[]{:S(2)}) %all-to-all-start.1) | async-done | bytes 2097184 | tf_op jit(solution)/shard_map/all_to_all | solution.py:38
  56.2 1.3 copy-done.2
  57.5 3.3 %fusion.18 = f32[1024,512]{0,1:T(8,128)S(1)} fusion(bf16[1024,1024]{1,0:T(8,128)(2,1)} %bitcast.36, bf16[1024,512]{1,0:T(8,128)(2,1)} %param.8), kind=kOutput, calls=%fused_computation.45 | convolution fusion | flops 1073741824 | bytes 5242880 | tf_op jit(solution)/shard_map/dot_general | solution.py:79
  60.8 1.3 fusion.17
  62.2 1.3 fusion.1
  63.4 0.3 copy-done.1
  63.8 3.5 %collective-permute-start = (bf16[512,1024]{0,1:T(8,128)(2,1)}, bf16[512,1024]{0,1:T(8,128)(2,1)}, u32[]{:S(2)}, u32[]{:S(2)}) collective-permute-start(bf16[512,1024]{0,1:T(8,128)(2,1)} %fusion.1), channel_id=1, source_target_pairs={{0,32},{32,0},{1,33},{33,1},{2,34},{34,2},{3,35},{35,3},{4,36},{36... | collective-permute-start | bytes 3145736 | tf_op jit(solution)/shard_map/ppermute | solution.py:47
  67.3 2.6 collective-permute-done
  69.9 1.7 copy_bitcast_fusion
  71.6 18.1 %all_to_all.95 = bf16[4,128,1024]{1,2,0:T(8,128)(2,1)S(1)} all-to-all(bf16[4,128,1024]{1,2,0:T(8,128)(2,1)S(1)} %copy_bitcast_fusion), channel_id=1, replica_groups=mesh['x'=4,'core'=2,'z'=8,'y'=4] {'x'}, dimensions={0} | all-to-all | bytes 2097152 | tf_op jit(solution)/shard_map/all_to_all | solution.py:20
  89.7 0.1 convert_reduce_fusion
  89.8 0.0 copy-start.5
  89.8 0.8 copy-done.5
  90.6 0.1 multiply_convert_fusion.2
  90.7 0.1 copy.28
  90.9 10.2 %all_to_all.96 = bf16[4,128,512]{2,1,0:T(8,128)(2,1)S(1)} all-to-all(bf16[4,128,512]{2,1,0:T(8,128)(2,1)S(1)} %broadcast_in_dim.9), channel_id=1, replica_groups=mesh['x'=4,'core'=2,'z'=8,'y'=4] {'x'}, dimensions={0} | all-to-all | bytes 1048576 | tf_op jit(solution)/shard_map/all_to_all | solution.py:20
  101.0 2.7 collective-permute-start.1
  103.7 1.5 collective-permute-done.1
  105.2 0.1 broadcast_select_fusion.3
  105.4 1.3 convolution_convert_fusion
  106.7 28.5 %all_to_all.97 = bf16[4,256,1024]{2,1,0:T(8,128)(2,1)S(1)} all-to-all(bf16[4,256,1024]{2,1,0:T(8,128)(2,1)S(1)} %bitcast.48), channel_id=1, replica_groups=mesh['x'=4,'core'=2,'z'=8,'y'=4] {'y'}, dimensions={0} | all-to-all | bytes 4194304 | tf_op jit(solution)/shard_map/all_to_all | solution.py:20
  135.2 1.3 reduce_sum.64
  136.5 3.5 %all-to-all-start.5 = ((bf16[8,32,1024]{2,1,0:T(8,128)(2,1)}), bf16[8,32,1024]{2,1,0:T(8,128)(2,1)S(1)}, u32[]{:S(2)}, u32[]{:S(2)}) async-start(bf16[8,32,1024]{2,1,0:T(8,128)(2,1)} %bitcast.49), calls=%async_computation.5 | async-start | bytes 1048576 | tf_op jit(solution)/shard_map/all_to_all | solution.py:20
  140.0 16.9 %all-to-all-done.5 = bf16[8,32,1024]{2,1,0:T(8,128)(2,1)S(1)} async-done(((bf16[8,32,1024]{2,1,0:T(8,128)(2,1)}), bf16[8,32,1024]{2,1,0:T(8,128)(2,1)S(1)}, u32[]{:S(2)}, u32[]{:S(2)}) %all-to-all-start.5) | async-done | bytes 524320 | tf_op jit(solution)/shard_map/all_to_all | solution.py:20
  156.9 0.1 convert_reduce_fusion.2
  157.0 1.5 subtract_convert_fusion
  158.6 18.1 %all_to_all.98 = bf16[8,32,1024]{2,1,0:T(8,128)(2,1)S(1)} all-to-all(bf16[8,32,1024]{2,1,0:T(8,128)(2,1)S(1)} %broadcast_in_dim.10), channel_id=1, replica_groups=mesh['x'=4,'core'=2,'z'=8,'y'=4] {'z'}, dimensions={0} | all-to-all | bytes 1048576 | tf_op jit(solution)/shard_map/all_to_all | solution.py:20
  176.7 0.3 stack.21
  176.9 25.9 %all_to_all.99 = bf16[4,256,1024]{2,1,0:T(8,128)(2,1)S(1)} all-to-all(bf16[4,256,1024]{2,1,0:T(8,128)(2,1)S(1)} %stack.21), channel_id=1, replica_groups=mesh['x'=4,'core'=2,'z'=8,'y'=4] {'y'}, dimensions={0} | all-to-all | bytes 4194304 | tf_op jit(solution)/shard_map/all_to_all | solution.py:38
  202.8 1.3 fusion.19
  204.1 0.0 copy-done.7
  204.1 0.1 dynamic-slice_convert_fusion
  204.2 0.0 copy-start.6
  204.2 4.0 %collective-permute-start.2 = (bf16[512,512]{1,0:T(8,128)(2,1)S(1)}, bf16[512,512]{1,0:T(8,128)(2,1)S(1)}, u32[]{:S(2)}, u32[]{:S(2)}) collective-permute-start(bf16[512,512]{1,0:T(8,128)(2,1)S(1)} %dynamic-slice_convert_fusion), channel_id=1, source_target_pairs={{0,32},{32,0},{1,33},{33,1},{2,34},{34,2},{3,35},{35,3},{4,36},{36... | collective-permute-start | bytes 1572872 | tf_op jit(solution)/shard_map/ppermute | solution.py:47
  208.2 1.5 collective-permute-done.2
  209.7 0.2 add_convert_fusion.1
  209.9 11.6 %all_to_all.100 = bf16[4,128,512]{2,1,0:T(8,128)(2,1)S(1)} all-to-all(bf16[4,128,512]{2,1,0:T(8,128)(2,1)S(1)} %bitcast.43), channel_id=1, replica_groups=mesh['x'=4,'core'=2,'z'=8,'y'=4] {'x'}, dimensions={0} | all-to-all | bytes 1048576 | tf_op jit(solution)/shard_map/all_to_all | solution.py:20
  221.5 0.1 convert_reduce_fusion.1
  221.6 0.1 copy.29
  221.7 0.2 multiply_convert_fusion.1
  221.9 0.1 copy.31
  222.1 0.1 broadcast_in_dim.11
  222.2 16.4 %all_to_all.101 = bf16[4,128,1024]{2,1,0:T(8,128)(2,1)S(1)} all-to-all(bf16[4,128,1024]{2,1,0:T(8,128)(2,1)S(1)} %broadcast_in_dim.11), channel_id=1, replica_groups=mesh['x'=4,'core'=2,'z'=8,'y'=4] {'x'}, dimensions={0} | all-to-all | bytes 2097152 | tf_op jit(solution)/shard_map/all_to_all | solution.py:20
  238.6 2.1 collective-permute-start.3
  240.7 2.3 collective-permute-done.3
  243.0 0.2 broadcast_select_fusion.1
  243.2 0.0 copy-start.10
  243.2 1.3 fusion.10
  244.5 1.3 add_convert_fusion
  245.8 29.3 %all_to_all.102 = bf16[4,256,1024]{2,1,0:T(8,128)(2,1)} all-to-all(bf16[4,256,1024]{2,1,0:T(8,128)(2,1)S(1)} %bitcast.40), channel_id=1, replica_groups=mesh['x'=4,'core'=2,'z'=8,'y'=4] {'y'}, dimensions={0} | all-to-all | bytes 4194304 | tf_op jit(solution)/shard_map/all_to_all | solution.py:20
  275.1 3.0 reduce_sum.67
  278.0 4.1 %all-to-all-start.11 = ((bf16[8,32,1024]{2,1,0:T(8,128)(2,1)}), bf16[8,32,1024]{2,1,0:T(8,128)(2,1)}, u32[]{:S(2)}, u32[]{:S(2)}) async-start(bf16[8,32,1024]{2,1,0:T(8,128)(2,1)} %bitcast.50), calls=%async_computation.11 | async-start | bytes 1048576 | tf_op jit(solution)/shard_map/all_to_all | solution.py:20
  282.2 4.3 %convolution_convert_fusion.1 = bf16[512,1024]{1,0:T(8,128)(2,1)} fusion(bf16[1024,1024]{1,0:T(8,128)(2,1)} %bitcast.47, bf16[512,512]{1,0:T(8,128)(2,1)} %copy-done.12, bf16[512,512]{1,0:T(8,128)(2,1)} %copy-done.11), kind=kOutput, calls=%fused_computation.14 | convolution fusion | flops 1076363264 | bytes 4194304 | tf_op jit(solution)/shard_map/dot_general | solution.py:12
  286.5 2.2 fusion.6
  288.7 2.3 copy.33
  291.0 3.8 %fusion.5 = bf16[1024,512]{0,1:T(8,128)(2,1)} fusion(bf16[1024,1024]{1,0:T(8,128)(2,1)} %bitcast.37, bf16[512,1024]{1,0:T(8,128)(2,1)S(1)} %get-tuple-element.25, bf16[512,1024]{1,0:T(8,128)(2,1)S(1)} %get-tuple-element.26), kind=kOutput, calls=%fused_computation.17 | convolution fusion | flops 1076363264 | bytes 5242880 | tf_op jit(solution)/shard_map/dot_general | solution.py:12
  294.9 2.3 copy.32
  297.1 2.1 all-to-all-done.11
  299.2 1.8 reduce_sum.68
  (21 shorter events, 0.1 us)
Async XLA Ops:
  0.6 104.7 %copy-start = (bf16[512,1024]{1,0:T(8,128)(2,1)S(1)}, bf16[512,1024]{1,0:T(8,128)(2,1)}, u32[]{:S(2)}) copy-start(bf16[512,1024]{1,0:T(8,128)(2,1)} %param.9) | copy-start | bytes 3145732
  28.2 28.0 %all-to-all-start.1 = ((bf16[4,256,1024]{2,1,0:T(8,128)(2,1)}), bf16[4,256,1024]{2,1,0:T(8,128)(2,1)S(1)}, u32[]{:S(2)}, u32[]{:S(2)}) async-start(bf16[4,256,1024]{2,1,0:T(8,128)(2,1)} %stack.9), calls=%async_computation.1 | async-start | bytes 4194304 | tf_op jit(solution)/shard_map/all_to_all | solution.py:38
  56.2 1.3 copy-start.2
  57.5 3.3 %copy-start.3 = (bf16[4,256,1024]{2,1,0:T(8,128)(2,1)S(1)}, bf16[4,256,1024]{2,1,0:T(8,128)(2,1)}, u32[]{:S(2)}) copy-start(bf16[4,256,1024]{2,1,0:T(8,128)(2,1)} %copy-done.2) | copy-start | bytes 6291460
  57.5 3.3 %copy-start.9 = (bf16[1024,512]{1,0:T(8,128)(2,1)S(1)}, bf16[1024,512]{1,0:T(8,128)(2,1)}, u32[]{:S(2)}) copy-start(bf16[1024,512]{1,0:T(8,128)(2,1)} %param.7) | copy-start | bytes 3145732
  62.1 1.6 copy-start.1
  63.8 6.1 %collective-permute-start = (bf16[512,1024]{0,1:T(8,128)(2,1)}, bf16[512,1024]{0,1:T(8,128)(2,1)}, u32[]{:S(2)}, u32[]{:S(2)}) collective-permute-start(bf16[512,1024]{0,1:T(8,128)(2,1)} %fusion.1), channel_id=1, source_target_pairs={{0,32},{32,0},{1,33},{33,1},{2,34},{34,2},{3,35},{35,3},{4,36},{36... | collective-permute-start | bytes 3145736 | tf_op jit(solution)/shard_map/ppermute | solution.py:47
  89.8 0.8 copy-start.5
  101.0 4.2 %collective-permute-start.1 = (bf16[512,512]{1,0:T(8,128)(2,1)S(1)}, bf16[512,512]{1,0:T(8,128)(2,1)S(1)}, u32[]{:S(2)}, u32[]{:S(2)}) collective-permute-start(bf16[512,512]{1,0:T(8,128)(2,1)S(1)} %bitcast.42), channel_id=1, source_target_pairs={{0,32},{32,0},{1,33},{33,1},{2,34},{34,2},{3,35},{35,3},{4,36},{36... | collective-permute-start | bytes 1572872 | tf_op jit(solution)/shard_map/ppermute | solution.py:47
  105.4 1.3 copy-start.11
  105.4 1.3 copy-start.12
  136.5 20.5 %all-to-all-start.5 = ((bf16[8,32,1024]{2,1,0:T(8,128)(2,1)}), bf16[8,32,1024]{2,1,0:T(8,128)(2,1)S(1)}, u32[]{:S(2)}, u32[]{:S(2)}) async-start(bf16[8,32,1024]{2,1,0:T(8,128)(2,1)} %bitcast.49), calls=%async_computation.5 | async-start | bytes 1048576 | tf_op jit(solution)/shard_map/all_to_all | solution.py:20
  202.8 1.3 copy-start.7
  204.2 17.5 %copy-start.6 = (f32[128,1024]{0,1:T(8,128)S(1)}, f32[128,1024]{0,1:T(8,128)}, u32[]{:S(2)}) copy-start(f32[128,1024]{0,1:T(8,128)} %copy-done.5) | copy-start | bytes 1572868
  204.2 5.5 %collective-permute-start.2 = (bf16[512,512]{1,0:T(8,128)(2,1)S(1)}, bf16[512,512]{1,0:T(8,128)(2,1)S(1)}, u32[]{:S(2)}, u32[]{:S(2)}) collective-permute-start(bf16[512,512]{1,0:T(8,128)(2,1)S(1)} %dynamic-slice_convert_fusion), channel_id=1, source_target_pairs={{0,32},{32,0},{1,33},{33,1},{2,34},{34,2},{3,35},{35,3},{4,36},{36... | collective-permute-start | bytes 1572872 | tf_op jit(solution)/shard_map/ppermute | solution.py:47
  238.6 4.6 %copy-start.8 = (bf16[1024,512]{1,0:T(8,128)(2,1)S(1)}, bf16[1024,512]{1,0:T(8,128)(2,1)}, u32[]{:S(2)}) copy-start(bf16[1024,512]{1,0:T(8,128)(2,1)} %param.8) | copy-start | bytes 3145732
  238.6 4.4 %collective-permute-start.3 = (bf16[512,1024]{1,0:T(8,128)(2,1)S(1)}, bf16[512,1024]{1,0:T(8,128)(2,1)S(1)}, u32[]{:S(2)}, u32[]{:S(2)}) collective-permute-start(bf16[512,1024]{1,0:T(8,128)(2,1)S(1)} %bitcast.41), channel_id=1, source_target_pairs={{0,32},{32,0},{1,33},{33,1},{2,34},{34,2},{3,35},{35,3},{4,36},{36... | collective-permute-start | bytes 3145736 | tf_op jit(solution)/shard_map/ppermute | solution.py:47
  243.2 1.3 copy-start.10
  278.0 21.2 %all-to-all-start.11 = ((bf16[8,32,1024]{2,1,0:T(8,128)(2,1)}), bf16[8,32,1024]{2,1,0:T(8,128)(2,1)}, u32[]{:S(2)}, u32[]{:S(2)}) async-start(bf16[8,32,1024]{2,1,0:T(8,128)(2,1)} %bitcast.50), calls=%async_computation.11 | async-start | bytes 1048576 | tf_op jit(solution)/shard_map/all_to_all | solution.py:20
  282.2 4.3 %copy-start.4 = (bf16[4,256,1024]{2,1,0:T(8,128)(2,1)S(1)}, bf16[4,256,1024]{2,1,0:T(8,128)(2,1)}, u32[]{:S(2)}) copy-start(bf16[4,256,1024]{2,1,0:T(8,128)(2,1)} %copy-done.2) | copy-start | bytes 6291460
